TPU v7x, 32 devices: a whole 2x2x4 slice. The times are simulated.
32 devices in a mesh: cfg: 2 (over y), space: 8 (over z, x), tm: 2 (over core).
Axes of the slice: x: 2, y: 2, z: 4, core: 2. Of those that a mesh axis runs over, the one named last changes fastest.
Arguments:
- eigvecs: bfloat16 [4, 2, 3, 1536, 256], P(('cfg', 'tm'), None, None, 'space'), parts along dimension 0, may hold values from -6 to 6
- momenta: int32 [3, 3], replicated, may hold values from -2 to 2, as said below
- pair_list: int32 [8, 2], P('tm'), may hold values from 0 to 1
- panels: bfloat16 [16, 2, 1024, 1024], P(('cfg', 'tm'), None, 'space'), parts along dimension 0, may hold values from -6 to 6
Outputs:
- dressed: bfloat16 [16, 3, 2, 1024, 1024], P(('cfg', 'tm'), None, None, 'space'), parts along dimension 0
There are 2 independent parts, one for each index of `cfg`. A program takes and returns all parts, laid end to end along the dimension named above; an argument that names none is the same for every part. Nothing has to cross between parts.
Inputs may be any that keep to these rules, and one draw needn't show every extreme that they name: `momenta`: the first component of every momentum is nonzero.
All inputs are finite; a program needn't handle non-finite values.
Results may differ from a plain program's by a relative error of at most 0.0075.
Values may be sent and summed in bfloat16 or wider, within the bound.
A program may use at most 64 MiB of HBM per device.

v0:
```python
import math
import jax
import jax.numpy as jnp
from jax import lax
from jax.sharding import PartitionSpec as P

LX = 64


def phased_block(cosine, sine_part, real_part, imag_part):
    cos_col = cosine[:, None]
    sin_col = sine_part[:, None]
    wave_re = cos_col * real_part + sin_col * imag_part
    wave_im = cos_col * imag_part - sin_col * real_part
    upper = jnp.concatenate([wave_re, wave_im], -1)
    lower = jnp.concatenate([wave_im, -wave_re], -1)
    return jnp.stack([upper, lower], -4).astype(jnp.bfloat16)


def local(eigvecs, momenta, pair_list, panels):
    slice_count, _, colors, slab_sites, vectors = eigvecs.shape
    mom_count = momenta.shape[0]
    space_count = lax.axis_size("space")
    first_site = lax.axis_index("space") * slab_sites
    site_index = first_site + jnp.arange(slab_sites, dtype=jnp.int32)
    xpos = site_index % LX
    ypos = site_index // LX % LX
    zpos = site_index // (LX * LX)
    wave = (
        momenta[:, 0:1] * xpos[None, :]
        + momenta[:, 1:2] * ypos[None, :]
        + momenta[:, 2:3] * zpos[None, :]
    )
    wave = jnp.mod(wave, LX)
    angle = wave.astype(jnp.float32) * jnp.float32(2.0 * math.pi / LX)
    cosine = jnp.cos(angle)
    sine_part = jnp.sin(angle)
    factor = 1.0 / math.sqrt(6.0 * slab_sites * space_count * vectors)
    real_part = eigvecs[:, 0].astype(jnp.float32)
    imag_part = eigvecs[:, 1].astype(jnp.float32)
    phased_all = jnp.concatenate(
        [
            phased_block(cosine[moment], sine_part[moment], real_part, imag_part)
            for moment in range(mom_count)
        ],
        -1,
    )
    phased_all = phased_all.reshape(slice_count, 2, colors, slab_sites, mom_count, 2 * vectors)
    gram_local = jnp.einsum(
        "trcsk,trcsml->tmkl", eigvecs, phased_all, preferred_element_type=jnp.float32
    )
    gram_local = factor * gram_local
    summed = lax.psum(gram_local, "space")
    own_fields = summed.astype(jnp.bfloat16)
    meson_fields = lax.all_gather(own_fields, "tm", axis=0, tiled=True)
    pair_count = pair_list.shape[0]
    panel_rows = panels.shape[2]
    panel_width = panels.shape[3]
    spins = panel_width // vectors
    source_fields = jnp.take(meson_fields, pair_list[:, 0], axis=0).reshape(
        pair_count, mom_count, vectors, 2, vectors
    )
    sink_fields = jnp.take(meson_fields, pair_list[:, 1], axis=0).reshape(
        pair_count, mom_count, vectors, 2, vectors
    )
    panel_parts = panels.reshape(pair_count, 2, panel_rows, spins, vectors)
    panel_re = panel_parts[:, 0]
    panel_im = panel_parts[:, 1]
    panel_mix = jnp.stack(
        [jnp.stack([panel_re, panel_im], 1), jnp.stack([panel_im, -panel_re], 1)], 1
    )
    right_dressed = jnp.einsum(
        "porxbk,pmlrk->pmoxbl", panel_mix, source_fields, preferred_element_type=jnp.float32
    )
    right_dressed = right_dressed.astype(jnp.bfloat16).reshape(
        pair_count * mom_count, 2, panel_rows, panel_width
    )
    turned = lax.all_to_all(right_dressed, "space", split_axis=3, concat_axis=2, tiled=True)
    column_count = turned.shape[3]
    turned = turned.reshape(pair_count, mom_count, 2, spins, vectors, column_count)
    turned_re = turned[:, :, 0]
    turned_im = turned[:, :, 1]
    mixed_parts = jnp.stack(
        [jnp.stack([turned_re, -turned_im], 2), jnp.stack([turned_im, turned_re], 2)], 2
    )
    dressed = jnp.einsum(
        "pmorajc,pmkrj->pmocak", mixed_parts, sink_fields, preferred_element_type=jnp.float32
    )
    return dressed.reshape(pair_count, mom_count, 2, column_count, panel_width).astype(jnp.bfloat16)


def solution(mesh):
    placed = (
        P(("cfg", "tm"), None, None, "space", None),
        P(),
        P("tm", None),
        P(("cfg", "tm"), None, "space", None),
    )
    return jax.shard_map(
        local,
        mesh=mesh,
        in_specs=placed,
        out_specs=P(("cfg", "tm"), None, None, "space", None),
        check_vma=False,
    )
```

profile of v0, /device:TPU:0, one launch (start us, length us, event | category | flops | bytes accessed | tf_op | source)
XLA Modules:
  0.0 343.8 jit_solution(5193341892418195743)
XLA Ops:
  6.5 0.0 all-gather.2.cloned.1.call-start
  6.6 1.0 slice_reduce_fusion.2
  7.6 0.1 fusion.37
  7.7 0.0 copy-start.3
  7.8 1.6 fusion.30
  9.3 0.1 maximum_bitcast_fusion.9
  9.4 0.1 pad_maximum_fusion
  9.5 0.0 copy-done.3
  9.6 0.3 fusion.28
  9.8 0.1 maximum_bitcast_fusion.11
  10.0 0.1 maximum_bitcast_fusion.13
  10.1 1.2 fusion.17
  11.3 83.3 %all-reduce.1 = bf16[1,3,256,512]{2,3,1,0:T(8,128)(2,1)S(1)} all-reduce(f32[1,3,256,512]{2,3,1,0:T(8,128)S(1)} %fusion.17), channel_id=1, replica_groups=mesh['cfg'=2,'space'=8,'tm'=2] {'space'}, use_global_device_ids=true, to_apply=%region_0.1 | all-reduce | flops 393216 | bytes 2359296 | tf_op jit(solution)/shard_map/psum | solution.py:53
  94.7 1.3 copy.48
  95.9 0.0 all-gather.2.cloned.1.call-update
  95.9 3.0 copy.49
  99.0 1.5 fusion.42
  100.4 1.5 copy.77
  102.0 1.2 neg.44
  103.2 0.0 copy-start.4
  103.2 0.0 copy-start.2
  103.2 2.4 copy.76
  105.6 2.3 copy.53
  107.9 0.0 copy-done.4
  107.9 0.0 copy-done.2
  107.9 2.7 maximum_bitcast_fusion.6
  110.7 0.0 all-gather.2.cloned.1.call-done
  110.7 2.2 gather_fusion.1
  112.8 2.0 broadcast_select_fusion
  114.9 3.8 %reshape.415 = bf16[4,3,256,2,256]{4,3,2,1,0:T(2,128)(2,1)S(1)} reshape(bf16[4,3,256,512]{3,2,1,0:T(8,128)(2,1)} %broadcast_select_fusion) | data formatting | bytes 6291456 | tf_op jit(solution)/shard_map/reshape | solution.py:60
  118.6 6.2 %bitcast_convert_fusion.1 = bf16[4,3,256,2,128,4]{4,2,5,3,1,0:T(8,128)(2,1)S(1)} fusion(bf16[4,1,2,128,4,256]{5,3,2,4,1,0:T(8,128)(2,1)} %maximum_bitcast_fusion.6, bf16[4,1,2,128,4,256]{5,3,2,4,1,0:T(8,128)(2,1)} %copy.53, bf16[4,3,256,2,256,1,1]{4,3,2,1,0,6,5:T(2,128)(2,1)S(1)} %bitcast.120), kind=kOutput, calls=%fused_computation.7 | convolution fusion | flops 3232759808 | bytes 13631488 | tf_op jit(solution)/shard_map/porxbk,pmlrk->pmoxbl/dot_general | solution.py:72
  124.8 36.6 %copy.55 = bf16[12,2,128,1024]{2,1,0,3:T(2,128)(2,1)} copy(bf16[12,2,128,1024]{2,3,1,0:T(8,128)(2,1)S(1)} %bitcast.117) | data formatting | bytes 12582912 | tf_op jit(solution)/shard_map/reshape | solution.py:75
  161.5 0.0 copy-start.1
  161.5 5.1 %all-to-all-start = ((bf16[12,2,128,1024]{2,1,0,3:T(2,128)(2,1)}), bf16[12,2,128,1024]{2,1,0,3:T(2,128)(2,1)}, u32[]{:S(2)}, u32[]{:S(2)}) async-start(bf16[12,2,128,1024]{2,1,0,3:T(2,128)(2,1)} %copy.55), calls=%async_computation | async-start | bytes 12582912 | tf_op jit(solution)/shard_map/all_to_all | solution.py:78
  166.5 0.0 copy-done.1
  166.6 2.5 gather_fusion
  169.0 2.3 broadcast_select_fusion.1
  171.3 3.1 reshape.414
  174.3 125.2 %all-to-all-done = bf16[12,2,128,1024]{2,1,0,3:T(2,128)(2,1)} async-done(((bf16[12,2,128,1024]{2,1,0,3:T(2,128)(2,1)}), bf16[12,2,128,1024]{2,1,0,3:T(2,128)(2,1)}, u32[]{:S(2)}, u32[]{:S(2)}) %all-to-all-start) | async-done | bytes 6291488 | tf_op jit(solution)/shard_map/all_to_all | solution.py:78
  299.6 6.9 %copy.56 = bf16[12,2,128,1024]{2,3,1,0:T(8,128)(2,1)} copy(bf16[12,2,128,1024]{2,1,0,3:T(2,128)(2,1)} %all-to-all-done) | data formatting | bytes 12582912 | tf_op jit(solution)/shard_map/all_to_all | solution.py:78
  306.4 8.6 %copy.57 = bf16[12,2,8,128,128]{4,3,2,1,0:T(8,128)(2,1)} copy(bf16[12,2,8,128,128]{3,4,2,1,0:T(8,128)(2,1)} %bitcast.114) | data formatting | bytes 12582912 | tf_op jit(solution)/shard_map/all_to_all | solution.py:78
  315.1 0.0 copy-start
  315.1 3.4 slice_bitcast_fusion
  318.5 1.2 copy-done
  319.7 0.4 fusion.41
  320.1 1.0 maximum_bitcast_fusion
  321.1 7.2 %bitcast_convert_fusion = bf16[4,3,256,2,4,128]{5,2,4,3,1,0:T(8,128)(2,1)} fusion(bf16[4,3,1,2,4,256,128]{6,5,3,4,2,1,0:T(8,128)(2,1)S(1)} %get-tuple-element.16, bf16[4,3,1,2,4,256,128]{6,5,3,4,2,1,0:T(8,128)(2,1)S(1)} %get-tuple-element.15, bf16[4,3,256,2,256,1,1]{4,3,2,1,0,6,5:T(2,128)(2,1)} %bitcast.119), kind=kOutput, calls=%fused_computation.6 | convolution fusion | flops 3249537024 | bytes 22020096 | tf_op jit(solution)/shard_map/pmorajc,pmkrj->pmocak/dot_general | solution.py:86
  328.3 8.6 %copy.62 = bf16[4,3,2,128,1024]{4,3,2,1,0:T(8,128)(2,1)} copy(bf16[4,3,2,128,1024]{3,4,2,1,0:T(8,128)(2,1)} %bitcast.118) | data formatting | bytes 12582912 | tf_op jit(solution)/shard_map/convert_element_type | solution.py:89
  (6 shorter events, 0.1 us)
Async XLA Ops:
  6.5 104.1 %all-gather.2.cloned.1.call-start = ((), (), s32[]{:S(2)}) async-start(), calls=%async_computation.1 | async-start | bytes 2359296 | tf_op jit(solution)/shard_map/all_gather | solution.py:55
  7.7 1.8 copy-start.3
  103.2 4.7 %copy-start.4 = (s32[4,2]{0,1:T(2,128)S(1)}, s32[4,2]{0,1:T(2,128)}, u32[]{:S(2)}) copy-start(s32[4,2]{0,1:T(2,128)} %param.8) | copy-start | bytes 100
  103.2 4.7 %copy-start.2 = (bf16[4,1,128,4,256]{4,2,1,3,0:T(8,128)(2,1)S(1)}, bf16[4,1,128,4,256]{4,2,1,3,0:T(8,128)(2,1)}, u32[]{:S(2)}) copy-start(bf16[4,1,128,4,256]{4,2,1,3,0:T(8,128)(2,1)} %neg.44) | copy-start | bytes 3145732
  161.5 5.1 %copy-start.1 = (bf16[2,3,256,512]{3,2,1,0:T(8,128)(2,1)S(1)}, bf16[2,3,256,512]{3,2,1,0:T(8,128)(2,1)}, u32[]{:S(2)}) copy-start(bf16[2,3,256,512]{3,2,1,0:T(8,128)(2,1)} %all-gather.2.cloned.1.call-done) | copy-start | bytes 4718596
  161.5 138.1 %all-to-all-start = ((bf16[12,2,128,1024]{2,1,0,3:T(2,128)(2,1)}), bf16[12,2,128,1024]{2,1,0,3:T(2,128)(2,1)}, u32[]{:S(2)}, u32[]{:S(2)}) async-start(bf16[12,2,128,1024]{2,1,0,3:T(2,128)(2,1)} %copy.55), calls=%async_computation | async-start | bytes 12582912 | tf_op jit(solution)/shard_map/all_to_all | solution.py:78
  315.1 4.6 %copy-start = (bf16[12,2,8,128,128]{4,3,2,1,0:T(8,128)(2,1)S(1)}, bf16[12,2,8,128,128]{4,3,2,1,0:T(8,128)(2,1)}, u32[]{:S(2)}) copy-start(bf16[12,2,8,128,128]{4,3,2,1,0:T(8,128)(2,1)} %copy.57) | copy-start | bytes 18874372
Sparse Core Ops, SparseCore 0:
  96.1 7.9 all-gather.1
where the time goes:
time: 345 us; the launch traced here: 344 us
  waiting for transfers between devices  125 us (36%)
  local copies, waits for them, and re-layouts  89.8 us (26%)
  blocking collectives  83.3 us (24%)
  matrix products  14.6 us (4%)
  between operations  13.6 us (4%)
  other arithmetic  12 us (3%)
  starting transfers between devices  5.08 us (1%)
    all_to_all x1, waiting for transfers between devices, local(): lax.all_to_all(right_dressed, 'space', split_axis=3, concat_axis=2, tiled...  125 us
    psum x1, blocking collectives, local(): summed = lax.psum(gram_local, 'space')  83.3 us
    reshape x1, local copies, waits for them, and re-layouts, local(): right_dressed.astype(jnp.bfloat16)  36.6 us
    all_to_all x2, local copies, waits for them, and re-layouts, local(): lax.all_to_all(right_dressed, 'space', split_axis=3, concat_axis=2, tiled...  15.5 us
    unnamed x14, local copies, waits for them, and re-layouts  11.6 us
    convert_element_type x1, local copies, waits for them, and re-layouts, local(): dressed.reshape(pair_count, mom_count, 2, column_count, panel_width)  8.62 us
    dot_general x1, matrix products, local(): jnp.einsum('pmorajc,pmkrj->pmocak', mixed_parts, sink_fields, preferred_e...  7.2 us
  transfers between devices with their start and end apart: 2, of which 1 were waited for; matrix products, arithmetic and copies ran while one was open for 7% of the time, Pallas kernels for 0%

commit v1 on v0

--- a/solution.py
+++ b/solution.py
@@ -50,7 +50,7 @@
         "trcsk,trcsml->tmkl", eigvecs, phased_all, preferred_element_type=jnp.float32
     )
     gram_local = factor * gram_local
-    summed = lax.psum(gram_local, "space")
+    summed = jnp.sum(lax.all_gather(gram_local, "space"), axis=0)
     own_fields = summed.astype(jnp.bfloat16)
     meson_fields = lax.all_gather(own_fields, "tm", axis=0, tiled=True)
     pair_count = pair_list.shape[0]

time: 345 us -> 453 us (1.31)
  waiting for transfers between devices: 125 us -> 309 us
  blocking collectives: 83.3 us -> 0 us
  other arithmetic: 12 us -> 18.4 us
    all_gather x0 -> x1, waiting for transfers between devices: none -> 179 us  [local(): summed = jnp.sum(lax.all_gather(gram_local, 'space'), axis=0)]
    psum x1 -> x0, blocking collectives: 83.3 us -> none  [local(): summed = lax.psum(gram_local, 'space')]
    reshape x2 -> x0, local copies, waits for them, and re-layouts: 6.8 us -> none  [the longest x1 3.75 us: local(): jnp.take(meson_fields, pair_list[:, 0], axis=0)]
    reduce_sum x0 -> x1, other arithmetic: none -> 6.3 us  [local(): summed = jnp.sum(lax.all_gather(gram_local, 'space'), axis=0)]
    select_n x0 -> x2, local copies, waits for them, and re-layouts: none -> 6.04 us  [the longest x1 3.17 us: local(): jnp.take(meson_fields, pair_list[:, 0], axis=0)]
    all_to_all x1, waiting for transfers between devices: 125 us -> 130 us  [local(): lax.all_to_all(right_dressed, 'space', split_axis=3, concat_axis=2, tiled...]
    unnamed x14 -> x15, local copies, waits for them, and re-layouts: 11.6 us -> 11.8 us
  transfers between devices with their start and end apart: 2 -> 3, of which waited for: 1 -> 2; matrix products, arithmetic and copies ran while one was open for 7% -> 5% of each run, Pallas kernels for 0% -> 0%
where the time goes in v1:
time: 453 us; the launch traced here: 452 us
  waiting for transfers between devices  309 us (68%)
  local copies, waits for them, and re-layouts  91 us (20%)
  other arithmetic  18.4 us (4%)
  matrix products  14.9 us (3%)
  between operations  13.6 us (3%)
  starting transfers between devices  5.34 us (1%)
    all_gather x1, waiting for transfers between devices, local(): summed = jnp.sum(lax.all_gather(gram_local, 'space'), axis=0)  179 us
    all_to_all x1, waiting for transfers between devices, local(): lax.all_to_all(right_dressed, 'space', split_axis=3, concat_axis=2, tiled...  130 us
    reshape x1, local copies, waits for them, and re-layouts, local(): right_dressed.astype(jnp.bfloat16)  36.6 us
    all_to_all x2, local copies, waits for them, and re-layouts, local(): lax.all_to_all(right_dressed, 'space', split_axis=3, concat_axis=2, tiled...  15.5 us
    unnamed x15, local copies, waits for them, and re-layouts  11.8 us
  transfers between devices with their start and end apart: 3, of which 2 were waited for; matrix products, arithmetic and copies ran while one was open for 5% of the time, Pallas kernels for 0%

profile of v1, /device:TPU:0, one launch (start us, length us, event | category | flops | bytes accessed | tf_op | source)
XLA Modules:
  0.0 452.0 jit_solution(7735838509833685711)
XLA Ops:
  6.5 0.0 all-gather.5.cloned.1.call-start
  6.6 1.0 slice_reduce_fusion.2
  7.6 0.1 fusion.35
  7.7 0.0 copy-start.3
  7.8 1.6 fusion.28
  9.3 0.1 maximum_bitcast_fusion.9
  9.4 0.1 pad_maximum_fusion
  9.5 0.0 copy-done.3
  9.6 0.3 fusion.26
  9.8 0.1 maximum_bitcast_fusion.11
  10.0 0.1 maximum_bitcast_fusion.13
  10.1 1.2 fusion.15
  11.3 1.6 copy.48
  12.9 0.0 all-gather.5.cloned.1.call-update
  12.9 0.2 all-gather.7.cloned.1.call-start
  13.2 178.7 %all-gather.5.cloned.1.call-done = f32[8,3,256,512]{3,2,1,0:T(8,128)} async-done(((f32[1,3,256,512]{3,2,1,0:T(8,128)}), f32[8,3,256,512]{3,2,1,0:T(8,128)}) %all-gather.5.cloned.1.call-update) | async-done | bytes 12582928 | tf_op jit(solution)/shard_map/all_gather | solution.py:53
  191.9 6.3 %reduce.1 = bf16[3,256,512]{2,1,0:T(8,128)(2,1)S(1)} reduce(f32[8,3,256,512]{3,2,1,0:T(8,128)} %all-gather.5.cloned.1.call-done, f32[]{:T(128)} %constant.75.clone.1), dimensions={0}, to_apply=%region_0.1 | reduce | flops 2752512 | bytes 13369348 | tf_op jit(solution)/shard_map/reduce_sum | solution.py:53
  198.2 0.3 copy.80
  198.5 1.2 copy.50
  199.7 0.0 all-gather.7.cloned.1.call-update
  199.8 3.0 copy.53
  202.8 1.5 fusion.40
  204.3 1.5 copy.82
  205.8 1.2 neg.44
  207.0 0.0 copy-start.4
  207.0 0.0 copy-start.2
  207.0 2.4 copy.81
  209.4 2.4 copy.57
  211.8 0.0 copy-done.4
  211.8 0.0 copy-done.2
  211.8 2.8 maximum_bitcast_fusion.6
  214.6 0.0 all-gather.7.cloned.1.call-done
  214.6 2.2 gather_fusion.1
  216.7 2.0 broadcast_select_fusion
  218.7 3.2 copy.52
  221.9 6.4 %bitcast_convert_fusion.1 = bf16[4,3,256,2,128,4]{4,2,5,3,1,0:T(8,128)(2,1)S(1)} fusion(bf16[4,3,256,2,256,1,1]{2,4,3,6,5,1,0:T(8,128)(2,1)S(1)} %bitcast.129, bf16[4,1,2,128,4,256]{5,3,2,4,1,0:T(8,128)(2,1)} %maximum_bitcast_fusion.6, bf16[4,1,2,128,4,256]{5,3,2,4,1,0:T(8,128)(2,1)} %copy.57), kind=kOutput, calls=%fused_computation.7 | convolution fusion | flops 3232759808 | bytes 13631488 | tf_op jit(solution)/shard_map/porxbk,pmlrk->pmoxbl/dot_general | solution.py:72
  228.3 36.6 %copy.59 = bf16[12,2,128,1024]{2,1,0,3:T(2,128)(2,1)} copy(bf16[12,2,128,1024]{2,3,1,0:T(8,128)(2,1)S(1)} %bitcast.126) | data formatting | bytes 12582912 | tf_op jit(solution)/shard_map/reshape | solution.py:75
  264.9 0.0 copy-start.1
  264.9 5.1 %all-to-all-start = ((bf16[12,2,128,1024]{2,1,0,3:T(2,128)(2,1)}), bf16[12,2,128,1024]{2,1,0,3:T(2,128)(2,1)}, u32[]{:S(2)}, u32[]{:S(2)}) async-start(bf16[12,2,128,1024]{2,1,0,3:T(2,128)(2,1)} %copy.59), calls=%async_computation | async-start | bytes 12582912 | tf_op jit(solution)/shard_map/all_to_all | solution.py:78
  270.0 0.0 copy-done.1
  270.0 2.5 gather_fusion
  272.5 2.3 broadcast_select_fusion.1
  274.8 2.9 copy.51
  277.6 130.0 %all-to-all-done = bf16[12,2,128,1024]{2,1,0,3:T(2,128)(2,1)} async-done(((bf16[12,2,128,1024]{2,1,0,3:T(2,128)(2,1)}), bf16[12,2,128,1024]{2,1,0,3:T(2,128)(2,1)}, u32[]{:S(2)}, u32[]{:S(2)}) %all-to-all-start) | async-done | bytes 6291488 | tf_op jit(solution)/shard_map/all_to_all | solution.py:78
  407.7 6.9 %copy.60 = bf16[12,2,128,1024]{2,3,1,0:T(8,128)(2,1)} copy(bf16[12,2,128,1024]{2,1,0,3:T(2,128)(2,1)} %all-to-all-done) | data formatting | bytes 12582912 | tf_op jit(solution)/shard_map/all_to_all | solution.py:78
  414.5 8.7 %copy.61 = bf16[12,2,8,128,128]{4,3,2,1,0:T(8,128)(2,1)} copy(bf16[12,2,8,128,128]{3,4,2,1,0:T(8,128)(2,1)} %bitcast.121) | data formatting | bytes 12582912 | tf_op jit(solution)/shard_map/all_to_all | solution.py:78
  423.2 0.0 copy-start
  423.2 3.4 slice_bitcast_fusion
  426.6 1.2 copy-done
  427.8 0.4 fusion.39
  428.2 1.0 maximum_bitcast_fusion
  429.2 7.3 %bitcast_convert_fusion = bf16[4,3,256,2,4,128]{5,2,4,3,1,0:T(8,128)(2,1)} fusion(bf16[4,3,256,2,256,1,1]{2,4,3,6,5,1,0:T(8,128)(2,1)} %bitcast.128, bf16[4,3,1,2,4,256,128]{6,5,3,4,2,1,0:T(8,128)(2,1)S(1)} %get-tuple-element.16, bf16[4,3,1,2,4,256,128]{6,5,3,4,2,1,0:T(8,128)(2,1)S(1)} %get-tuple-element.15), kind=kOutput, calls=%fused_computation.6 | convolution fusion | flops 3249537024 | bytes 22020096 | tf_op jit(solution)/shard_map/pmorajc,pmkrj->pmocak/dot_general | solution.py:86
  436.6 8.6 %copy.66 = bf16[4,3,2,128,1024]{4,3,2,1,0:T(8,128)(2,1)} copy(bf16[4,3,2,128,1024]{3,4,2,1,0:T(8,128)(2,1)} %bitcast.127) | data formatting | bytes 12582912 | tf_op jit(solution)/shard_map/convert_element_type | solution.py:89
  (6 shorter events, 0.1 us)
Async XLA Ops:
  6.5 185.4 %all-gather.5.cloned.1.call-start = ((), (), s32[]{:S(2)}) async-start(), calls=%async_computation.1 | async-start | bytes 14155776 | tf_op jit(solution)/shard_map/all_gather | solution.py:53
  7.7 1.8 copy-start.3
  12.9 201.6 %all-gather.7.cloned.1.call-start = ((), (), s32[]{:S(2)}) async-start(), calls=%async_computation.2 | async-start | bytes 2359296 | tf_op jit(solution)/shard_map/all_gather | solution.py:55
  207.0 4.7 %copy-start.4 = (s32[4,2]{0,1:T(2,128)S(1)}, s32[4,2]{0,1:T(2,128)}, u32[]{:S(2)}) copy-start(s32[4,2]{0,1:T(2,128)} %param.8) | copy-start | bytes 100
  207.0 4.8 %copy-start.2 = (bf16[4,1,128,4,256]{4,2,1,3,0:T(8,128)(2,1)S(1)}, bf16[4,1,128,4,256]{4,2,1,3,0:T(8,128)(2,1)}, u32[]{:S(2)}) copy-start(bf16[4,1,128,4,256]{4,2,1,3,0:T(8,128)(2,1)} %neg.44) | copy-start | bytes 3145732
  264.9 5.1 %copy-start.1 = (bf16[6,256,512]{2,1,0:T(8,128)(2,1)S(1)}, bf16[6,256,512]{2,1,0:T(8,128)(2,1)}, u32[]{:S(2)}) copy-start(bf16[6,256,512]{2,1,0:T(8,128)(2,1)} %all-gather.7.cloned.1.call-done) | copy-start | bytes 4718596
  264.9 142.7 %all-to-all-start = ((bf16[12,2,128,1024]{2,1,0,3:T(2,128)(2,1)}), bf16[12,2,128,1024]{2,1,0,3:T(2,128)(2,1)}, u32[]{:S(2)}, u32[]{:S(2)}) async-start(bf16[12,2,128,1024]{2,1,0,3:T(2,128)(2,1)} %copy.59), calls=%async_computation | async-start | bytes 12582912 | tf_op jit(solution)/shard_map/all_to_all | solution.py:78
  423.2 4.6 %copy-start = (bf16[12,2,8,128,128]{4,3,2,1,0:T(8,128)(2,1)S(1)}, bf16[12,2,8,128,128]{4,3,2,1,0:T(8,128)(2,1)}, u32[]{:S(2)}) copy-start(bf16[12,2,8,128,128]{4,3,2,1,0:T(8,128)(2,1)} %copy.61) | copy-start | bytes 18874372
Sparse Core Ops, SparseCore 0:
  13.1 178.8 all-gather.4
  199.9 7.9 all-gather.6
